TPU v7x, 32 devices: a whole 2x2x4 slice. The times are simulated.
32 devices in a mesh: dp: 4 (over z), seq: 4 (over y, x), expert: 2 (over core).
Axes of the slice: x: 2, y: 2, z: 4, core: 2. Of those that a mesh axis runs over, the one named last changes fastest.
Arguments:
- block_input: float32 [8, 512, 768], P(('dp', 'expert'), 'seq'), may hold values from -12 to 12
- documents: int32 [8, 512], P(('dp', 'expert')), may hold values from 0 to 2, never falling along the last dimension, each value on 1 to 320 neighbouring positions
- route_experts: int32 [8, 512, 2], P(('dp', 'expert'), 'seq'), may hold values from 0 to 7, all different within a row; in each aligned block of 128 rows (0 to 127, 128 to 255, ..., all dimensions but the last counted through in order) at most 48 rows name the same one
- route_gate: float32 [8, 512, 2], P(('dp', 'expert'), 'seq'), may hold values from 0.25 to 1
- first_gain: bfloat16 [768], P(('dp', 'seq', 'expert')), may hold values from 0.25 to 1.75
- entry_weight: bfloat16 [768, 2304], P(None, ('dp', 'seq', 'expert')), may hold values from -0.21875 to 0.21875
- exit_weight: bfloat16 [768, 768], P(None, ('dp', 'seq', 'expert')), may hold values from -0.875 to 0.875
- position_bias: float32 [32, 12], replicated, may hold values from -4 to 260
- second_gain: bfloat16 [768], P(('dp', 'seq', 'expert')), may hold values from 0.25 to 1.75
- expert_up: bfloat16 [8, 768, 3072], P(('dp', 'expert'), None, 'seq'), may hold values from -0.21875 to 0.21875
- expert_down: bfloat16 [8, 3072, 768], P(('dp', 'expert'), 'seq'), may hold values from -0.109375 to 0.109375
- cotangent: float32 [8, 512, 768], P(('dp', 'expert'), 'seq'), may hold values from -6 to 6
Outputs:
- block_output: float32 [8, 512, 768], P(('dp', 'expert'), 'seq')
- back_input: float32 [8, 512, 768], P(('dp', 'expert'), 'seq')
- back_first_gain: float32 [768], P(('dp', 'seq', 'expert'))
- back_entry: float32 [768, 2304], P(None, ('dp', 'seq', 'expert'))
- back_exit: float32 [768, 768], P(None, ('dp', 'seq', 'expert'))
- back_bias: float32 [32, 12], replicated
- back_second_gain: float32 [768], P(('dp', 'seq', 'expert'))
- back_expert_up: float32 [8, 768, 3072], P(('dp', 'expert'), None, 'seq')
- back_expert_down: float32 [8, 3072, 768], P(('dp', 'expert'), 'seq')
Inputs may be any that keep to these rules, and one draw needn't show every extreme that they name: `route_experts`: in each device's aligned block of 128 tokens no expert is named by more than 48 routes, a bound that some block reaches; a token's two experts differ. `documents`: document numbers never fall along a sequence; no document is longer than five eighths of 512 tokens, and one is that long.
All inputs are finite; a program needn't handle non-finite values.
Results may differ from a plain program's by a relative error of at most 0.014.
Values may be sent and summed in bfloat16 or wider, within the bound.
No kernel may reach another device: no remote copies, remote signals or barrier semaphores. Data moves between devices by JAX's collectives and lax.ppermute only.
A program may use at most 128 MiB of HBM per device.

v0:
```python
import jax
import jax.numpy as jnp
from jax import lax
from jax.sharding import PartitionSpec as P

EPSILON = 1e-06
SLOPE = 0.7978845608028654
CUBIC = 0.044715
LIMITS = (19, 21, 24, 27, 31, 35, 40, 46, 52, 59, 67, 77, 87, 99, 113)
MASKED = -1e30
HIGH = lax.Precision.HIGHEST


def gelu_value(values):
    return 0.5 * values * (1.0 + jnp.tanh(SLOPE * (values + CUBIC * values * values * values)))


def gelu_slope(values):
    tangent = jnp.tanh(SLOPE * (values + CUBIC * values * values * values))
    return 0.5 * (1.0 + tangent) + 0.5 * values * (1.0 - tangent * tangent) * SLOPE * (
        1.0 + 3.0 * CUBIC * values * values
    )


def bucket_onehot(lag, count):
    bucket = jnp.minimum(lag, 16)
    for threshold in LIMITS:
        bucket = bucket + (lag >= threshold).astype(jnp.int32)
    return (bucket[..., None] == jnp.arange(count, dtype=jnp.int32)).astype(jnp.float32)


def rms_scale(values):
    return lax.rsqrt(jnp.mean(values * values, axis=-1, keepdims=True) + EPSILON)


def contract_rows(left, right):
    return lax.dot_general(
        left, right, (((0,), (0,)), ((), ())), preferred_element_type=jnp.float32
    )


def contract_cols(left, right):
    return lax.dot_general(
        left, right, (((1,), (1,)), ((), ())), preferred_element_type=jnp.float32
    )


def masked_scores(queries, key_heads, bias_block, allowed, factor):
    scores = (
        jnp.einsum("qhd,khd->hqk", queries, key_heads, preferred_element_type=jnp.float32) * factor
        + bias_block
    )
    return jnp.where(allowed[None], scores, MASKED)


def expert_work(rows, upstream, up_weight, down_weight):
    before = jnp.dot(rows, up_weight, preferred_element_type=jnp.float32)
    active = gelu_value(before).astype(jnp.bfloat16)
    result = jnp.dot(active, down_weight, preferred_element_type=jnp.float32)
    back_active = contract_cols(upstream, down_weight)
    back_before = (back_active * gelu_slope(before)).astype(jnp.bfloat16)
    down_grad = contract_rows(active, upstream)
    up_grad = contract_rows(rows, back_before)
    back_rows = contract_cols(back_before, up_weight)
    return (result, back_rows, up_grad, down_grad)


def local(
    block_input,
    documents,
    route_experts,
    route_gate,
    first_gain,
    entry_weight,
    exit_weight,
    position_bias,
    second_gain,
    expert_up,
    expert_down,
    cotangent,
):
    rows_here = block_input.shape[1]
    features = block_input.shape[2]
    head_count = position_bias.shape[1]
    head_size = features // head_count
    factor = head_size ** (-0.5)
    top_count = route_experts.shape[2]
    inputs = block_input.reshape(rows_here, features)
    upstream = cotangent.reshape(rows_here, features)
    gain_one, entry_full, exit_full, gain_two = (
        lax.all_gather(first_gain, ("dp", "seq", "expert"), axis=0, tiled=True),
        lax.all_gather(entry_weight, ("dp", "seq", "expert"), axis=1, tiled=True),
        lax.all_gather(exit_weight, ("dp", "seq", "expert"), axis=1, tiled=True),
        lax.all_gather(second_gain, ("dp", "seq", "expert"), axis=0, tiled=True),
    )
    gain_one = gain_one.astype(jnp.float32)
    gain_two = gain_two.astype(jnp.float32)
    scale_one = rms_scale(inputs)
    normed_one = (inputs * scale_one * gain_one).astype(jnp.bfloat16)
    projected = jnp.dot(normed_one, entry_full, preferred_element_type=jnp.float32).astype(
        jnp.bfloat16
    )
    queries = projected[:, :features].reshape(rows_here, head_count, head_size)
    key_value = lax.all_gather(projected[:, features:], "seq", axis=0, tiled=True)
    seq_length = key_value.shape[0]
    key_heads = key_value[:, :features].reshape(seq_length, head_count, head_size)
    values = key_value[:, features:].reshape(seq_length, head_count, head_size)
    offset = lax.axis_index("seq") * rows_here
    query_index = offset + jnp.arange(rows_here, dtype=jnp.int32)
    key_index = jnp.arange(seq_length, dtype=jnp.int32)
    segment_keys = documents.reshape(seq_length)
    segment_queries = lax.dynamic_slice_in_dim(segment_keys, offset, rows_here)
    allowed = (key_index[None, :] <= query_index[:, None]) & (
        segment_queries[:, None] == segment_keys[None, :]
    )
    lag_table = jnp.maximum(query_index[:, None] - key_index[None, :], 0)
    bucket_hot = bucket_onehot(lag_table, position_bias.shape[0])
    bias_block = jnp.einsum("qkb,bh->hqk", bucket_hot, position_bias, precision=HIGH)
    scores = masked_scores(queries, key_heads, bias_block, allowed, factor)
    row_peak = jnp.max(scores, axis=2, keepdims=True)
    log_total = row_peak + jnp.log(jnp.sum(jnp.exp(scores - row_peak), axis=2, keepdims=True))
    weights = jnp.where(allowed[None], jnp.exp(scores - log_total), 0.0).astype(jnp.bfloat16)
    context = (
        jnp.einsum("hqk,khd->qhd", weights, values, preferred_element_type=jnp.float32)
        .astype(jnp.bfloat16)
        .reshape(rows_here, features)
    )
    hidden = inputs + jnp.dot(context, exit_full, preferred_element_type=jnp.float32)
    scale_two = rms_scale(hidden)
    normed_two = (hidden * scale_two * gain_two).astype(jnp.bfloat16)
    group_size = lax.axis_size(("dp", "expert"))
    capacity = 3 * rows_here // group_size
    route_count = rows_here * top_count
    flat_routes = route_experts.reshape(route_count)
    flat_gates = route_gate.reshape(route_count)
    member = (flat_routes[:, None] == jnp.arange(group_size, dtype=jnp.int32)[None, :]).astype(
        jnp.int32
    )
    route_rank = jnp.sum(member * (jnp.cumsum(member, axis=0) - 1), axis=1)
    slot_of = flat_routes * capacity + route_rank
    filler = (
        jnp.full((group_size * capacity,), -1, jnp.int32)
        .at[slot_of]
        .set(jnp.arange(route_count, dtype=jnp.int32))
    )
    present = filler >= 0
    source = jnp.maximum(filler, 0)
    token_of = source // top_count
    send_rows = jnp.where(present[:, None], normed_two[token_of], jnp.zeros((), jnp.bfloat16))
    send_upstream = jnp.where(
        present[:, None], upstream[token_of] * flat_gates[source][:, None], 0.0
    ).astype(jnp.bfloat16)
    shaped = (group_size, capacity, features)
    arrived_input, arrived_upstream = (
        lax.all_to_all(
            send_rows.reshape(shaped), ("dp", "expert"), split_axis=0, concat_axis=0, tiled=True
        ),
        lax.all_to_all(
            send_upstream.reshape(shaped), ("dp", "expert"), split_axis=0, concat_axis=0, tiled=True
        ),
    )
    rows_flat = arrived_input.reshape(group_size * capacity, features)
    upstream_flat = arrived_upstream.reshape(group_size * capacity, features)
    full_up, full_down = (
        lax.all_gather(expert_up, "seq", axis=2, tiled=True),
        lax.all_gather(expert_down, "seq", axis=1, tiled=True),
    )
    result, back_rows, up_grad, down_grad = expert_work(
        rows_flat, upstream_flat, full_up[0], full_down[0]
    )
    up_share, down_share = (
        lax.psum_scatter(
            up_grad[None].astype(jnp.bfloat16), "seq", scatter_dimension=2, tiled=True
        ).astype(jnp.float32),
        lax.psum_scatter(
            down_grad[None].astype(jnp.bfloat16), "seq", scatter_dimension=1, tiled=True
        ).astype(jnp.float32),
    )
    returned_out, returned_back = (
        lax.all_to_all(
            result.astype(jnp.bfloat16).reshape(shaped),
            ("dp", "expert"),
            split_axis=0,
            concat_axis=0,
            tiled=True,
        ),
        lax.all_to_all(
            back_rows.astype(jnp.bfloat16).reshape(shaped),
            ("dp", "expert"),
            split_axis=0,
            concat_axis=0,
            tiled=True,
        ),
    )
    route_out = (
        returned_out.reshape(group_size * capacity, features)[slot_of]
        .astype(jnp.float32)
        .reshape(rows_here, top_count, features)
    )
    mixture = jnp.sum(route_out * route_gate.reshape(rows_here, top_count, 1), axis=1)
    block_output = hidden + mixture
    route_back = (
        returned_back.reshape(group_size * capacity, features)[slot_of]
        .astype(jnp.float32)
        .reshape(rows_here, top_count, features)
    )
    back_normed_two = jnp.sum(route_back, axis=1)
    upper_two = back_normed_two * gain_two
    gain_two_grad = jnp.sum(back_normed_two * hidden * scale_two, axis=0)
    back_hidden = upstream + scale_two * (
        upper_two
        - hidden * scale_two * scale_two * jnp.mean(upper_two * hidden, axis=1, keepdims=True)
    )
    entry_back, exit_back = (
        lax.all_gather(entry_weight, ("dp", "seq", "expert"), axis=1, tiled=True),
        lax.all_gather(exit_weight, ("dp", "seq", "expert"), axis=1, tiled=True),
    )
    upstream_hidden = back_hidden.astype(jnp.bfloat16)
    exit_grad = contract_rows(context, upstream_hidden)
    back_context = (
        contract_cols(upstream_hidden, exit_back)
        .astype(jnp.bfloat16)
        .reshape(rows_here, head_count, head_size)
    )
    scores_again = masked_scores(queries, key_heads, bias_block, allowed, factor)
    probs = jnp.where(allowed[None], jnp.exp(scores_again - log_total), 0.0)
    back_probs = jnp.einsum(
        "qhd,khd->hqk", back_context, values, preferred_element_type=jnp.float32
    )
    row_dot = jnp.sum(probs * back_probs, axis=2, keepdims=True)
    back_scores = probs * (back_probs - row_dot)
    bias_grad = jnp.einsum("hqk,qkb->bh", back_scores, bucket_hot, precision=HIGH)
    scaled_back = (back_scores * factor).astype(jnp.bfloat16)
    back_queries = jnp.einsum(
        "hqk,khd->qhd", scaled_back, key_heads, preferred_element_type=jnp.float32
    ).reshape(rows_here, features)
    back_keys = jnp.einsum(
        "hqk,qhd->khd", scaled_back, queries, preferred_element_type=jnp.float32
    ).reshape(seq_length, features)
    back_values = jnp.einsum(
        "hqk,qhd->khd", probs.astype(jnp.bfloat16), back_context, preferred_element_type=jnp.float32
    ).reshape(seq_length, features)
    back_pairs = lax.psum_scatter(
        jnp.concatenate([back_keys, back_values], axis=1).astype(jnp.bfloat16),
        "seq",
        scatter_dimension=0,
        tiled=True,
    ).astype(jnp.float32)
    back_projected = jnp.concatenate([back_queries, back_pairs], axis=1).astype(jnp.bfloat16)
    entry_grad = contract_rows(normed_one, back_projected)
    back_normed_one = contract_cols(back_projected, entry_back)
    upper_one = back_normed_one * gain_one
    gain_one_grad = jnp.sum(back_normed_one * inputs * scale_one, axis=0)
    back_input = back_hidden + scale_one * (
        upper_one
        - inputs * scale_one * scale_one * jnp.mean(upper_one * inputs, axis=1, keepdims=True)
    )
    gain_one_share, entry_share, exit_share, gain_two_share = (
        lax.psum_scatter(gain_one_grad, ("dp", "seq", "expert"), scatter_dimension=0, tiled=True),
        lax.psum_scatter(entry_grad, ("dp", "seq", "expert"), scatter_dimension=1, tiled=True),
        lax.psum_scatter(exit_grad, ("dp", "seq", "expert"), scatter_dimension=1, tiled=True),
        lax.psum_scatter(gain_two_grad, ("dp", "seq", "expert"), scatter_dimension=0, tiled=True),
    )
    bias_total = lax.psum(bias_grad, ("dp", "seq", "expert"))
    return (
        block_output.reshape(block_input.shape),
        back_input.reshape(block_input.shape),
        gain_one_share,
        entry_share,
        exit_share,
        bias_total,
        gain_two_share,
        up_share,
        down_share,
    )


def solution(mesh):
    placed = (
        P(("dp", "expert"), "seq", None),
        P(("dp", "expert"), None),
        P(("dp", "expert"), "seq", None),
        P(("dp", "expert"), "seq", None),
        P(("dp", "seq", "expert")),
        P(None, ("dp", "seq", "expert")),
        P(None, ("dp", "seq", "expert")),
        P(),
        P(("dp", "seq", "expert")),
        P(("dp", "expert"), None, "seq"),
        P(("dp", "expert"), "seq", None),
        P(("dp", "expert"), "seq", None),
    )
    return jax.shard_map(
        local,
        mesh=mesh,
        in_specs=placed,
        out_specs=(
            P(("dp", "expert"), "seq", None),
            P(("dp", "expert"), "seq", None),
            P(("dp", "seq", "expert")),
            P(None, ("dp", "seq", "expert")),
            P(None, ("dp", "seq", "expert")),
            P(),
            P(("dp", "seq", "expert")),
            P(("dp", "expert"), None, "seq"),
            P(("dp", "expert"), "seq", None),
        ),
        check_vma=False,
    )
```

profile of v0, /device:TPU:0, one launch (start us, length us, event | category | flops | bytes accessed | tf_op | source)
XLA Modules:
  0.0 738.7 jit_solution(6812603287576350508)
XLA Ops:
  9.7 42.8 %all-reduce.5 = (bf16[768]{0:T(1024)(128)(2,1)S(1)}, bf16[768]{0:T(1024)(128)(2,1)S(1)}) all-reduce(bf16[768]{0:T(1024)(128)(2,1)S(1)} %dynamic-update-slice, bf16[768]{0:T(1024)(128)(2,1)S(1)} %dynamic-update-slice.1), channel_id=1, replica_groups=mesh['dp'=4,'seq'=4,'expert'=2] {'dp','seq','expert'}, use_global_device_ids=true, to_apply=%add | all-reduce | flops 1536 | bytes 6144
  53.6 20.0 %all-gather.6.cloned.1.call-done = bf16[768,2304]{0,1:T(8,128)(2,1)} async-done(((bf16[768,72]{0,1:T(8,128)(2,1)}), bf16[768,2304]{0,1:T(8,128)(2,1)}) %all-gather.6.cloned.1.call-update) | async-done | bytes 3538960 | tf_op jit(solution)/shard_map/all_gather | solution.py:92
  73.6 3.4 convolution_convert_fusion.2
  82.3 4.1 fusion.1
  86.4 3.5 copy.51
  95.3 13.1 %all-gather.8.cloned.1.call-done = bf16[512,1536]{1,0:T(8,128)(2,1)} async-done(((bf16[128,1536]{1,0:T(8,128)(2,1)}), bf16[512,1536]{1,0:T(8,128)(2,1)}) %all-gather.8.cloned.1.call-update) | async-done | bytes 1572880 | tf_op jit(solution)/shard_map/all_gather | solution.py:104
  120.2 45.1 %all-gather.10.cloned.1.call-done = bf16[768,768]{0,1:T(8,128)(2,1)} async-done(((bf16[768,24]{0,1:T(8,128)(2,1)}), bf16[768,768]{0,1:T(8,128)(2,1)}) %all-gather.10.cloned.1.call-update) | async-done | bytes 1179664 | tf_op jit(solution)/shard_map/all_gather | solution.py:93
  170.5 4.0 all-to-all-start
  180.6 10.6 %all-to-all-done = bf16[8,48,768]{2,1,0:T(8,128)(2,1)S(1)} async-done(((bf16[8,48,768]{2,1,0:T(8,128)(2,1)}), bf16[8,48,768]{2,1,0:T(8,128)(2,1)S(1)}, u32[]{:S(2)}, u32[]{:S(2)}) %all-to-all-start) | async-done | bytes 589856 | tf_op jit(solution)/shard_map/all_to_all | solution.py:155
  191.2 3.5 all-to-all-start.2
  194.8 28.1 %all-gather.12.cloned.1.call-done = bf16[1,768,3072]{2,1,0:T(8,128)(2,1)} async-done(((bf16[1,768,768]{2,1,0:T(8,128)(2,1)}), bf16[1,768,3072]{2,1,0:T(8,128)(2,1)}) %all-gather.12.cloned.1.call-update) | async-done | bytes 4718608 | tf_op jit(solution)/shard_map/all_gather | solution.py:165
  222.9 6.5 fusion.15
  229.4 52.1 %all-gather.14.cloned.1.call-done = bf16[1,3072,768]{2,1,0:T(8,128)(2,1)} async-done(((bf16[1,768,768]{2,1,0:T(8,128)(2,1)}), bf16[1,3072,768]{2,1,0:T(8,128)(2,1)}) %all-gather.14.cloned.1.call-update) | async-done | bytes 4718608 | tf_op jit(solution)/shard_map/all_gather | solution.py:166
  281.5 7.7 %fusion.8 = bf16[384,3072]{1,0:T(8,128)(2,1)S(1)} fusion(f32[384,3072]{1,0:T(8,128)} %fusion.15, bf16[384,768]{1,0:T(8,128)(2,1)S(1)} %bitcast.134, bf16[1,3072,768]{2,1,0:T(8,128)(2,1)} %all-gather.14.cloned.1.call-done), kind=kOutput, calls=%fused_computation.19 | convolution fusion | flops 1834352640 | bytes 12386304 | tf_op jit(solution)/shard_map/dot_general | solution.py:43
  289.2 2.9 fusion.25
  292.1 4.6 all-to-all-start.3
  296.7 7.4 %fusion.28 = bf16[384,768]{1,0:T(8,128)(2,1)} fusion(bf16[1,3072,768]{2,1,0:T(8,128)(2,1)} %all-gather.14.cloned.1.call-done, f32[384,3072]{1,0:T(8,128)} %fusion.15), kind=kOutput, calls=%fused_computation.46 | convolution fusion | flops 1822851072 | bytes 10027008 | tf_op jit(solution)/shard_map/dot_general | solution.py:59
  304.1 9.3 %all-to-all-done.3 = bf16[8,48,768]{2,1,0:T(8,128)(2,1)S(1)} async-done(((bf16[8,48,768]{2,1,0:T(8,128)(2,1)}), bf16[8,48,768]{2,1,0:T(8,128)(2,1)S(1)}, u32[]{:S(2)}, u32[]{:S(2)}) %all-to-all-start.3) | async-done | bytes 589856 | tf_op jit(solution)/shard_map/all_to_all | solution.py:187
  313.4 3.5 all-to-all-start.1
  321.7 11.9 %all-to-all-done.1 = bf16[8,48,768]{2,1,0:T(8,128)(2,1)S(1)} async-done(((bf16[8,48,768]{2,1,0:T(8,128)(2,1)}), bf16[8,48,768]{2,1,0:T(8,128)(2,1)S(1)}, u32[]{:S(2)}, u32[]{:S(2)}) %all-to-all-start.1) | async-done | bytes 589856 | tf_op jit(solution)/shard_map/all_to_all | solution.py:180
  350.9 6.0 fusion.17
  358.0 7.6 %fusion.18 = bf16[1,3072,768]{2,1,0:T(8,128)(2,1)} fusion(bf16[384,768]{1,0:T(8,128)(2,1)S(1)} %bitcast.135, f32[384,3072]{1,0:T(8,128)} %fusion.15), kind=kOutput, calls=%fused_computation.30 | convolution fusion | flops 1824915456 | bytes 10027008 | tf_op jit(solution)/shard_map/dot_general | solution.py:37
  366.6 3.0 fusion.57
  372.2 7.9 %reduce-scatter.16.cloned.1.call-done = bf16[128,1536]{1,0:T(8,128)(2,1)} async-done(((bf16[512,1536]{1,0:T(8,128)(2,1)}), bf16[128,1536]{1,0:T(8,128)(2,1)}) %reduce-scatter.16.cloned.1.call-update) | async-done | bytes 393232
  382.0 5.1 fusion.36
  387.2 3.6 copy.58
  390.8 6.3 fusion.31
  397.9 41.0 %all-reduce.4 = (f32[768]{0:T(1024)S(1)}, f32[32,12]{0,1:T(8,128)}, f32[768]{0:T(1024)S(1)}) all-reduce(f32[768]{0:T(1024)S(1)} %get-tuple-element.11, f32[32,12]{0,1:T(8,128)S(1)} %fusion.31, f32[768]{0:T(1024)S(1)} %copy-done.33), channel_id=3, replica_groups=mesh['dp'=4,'seq'=4,'expert'=2] {'dp','seq','expert'}, use_global_device_ids=true, to_apply=%region_15.16.clone | all-reduce | flops 1920 | bytes 15360
  441.4 2.8 convert_element_type.234
  444.3 57.2 %reduce-scatter.14.cloned.1.call-done = bf16[1,768,768]{2,1,0:T(8,128)(2,1)} async-done(((bf16[1,3072,768]{2,1,0:T(8,128)(2,1)}), bf16[1,768,768]{2,1,0:T(8,128)(2,1)}) %reduce-scatter.14.cloned.1.call-update) | async-done | bytes 1179664 | tf_op jit(solution)/shard_map/reduce_scatter | solution.py:175
  504.3 102.7 %reduce-scatter.10.cloned.1.call-done = f32[768,24]{0,1:T(8,128)} async-done(((f32[768,768]{0,1:T(8,128)}), f32[768,24]{0,1:T(8,128)}) %reduce-scatter.10.cloned.1.call-update) | async-done | bytes 73744 | tf_op jit(solution)/shard_map/reduce_scatter | solution.py:261
  607.0 124.6 %reduce-scatter.8.cloned.1.call-done = f32[768,72]{0,1:T(8,128)} async-done(((f32[768,2304]{0,1:T(8,128)}), f32[768,72]{0,1:T(8,128)}) %reduce-scatter.8.cloned.1.call-update) | async-done | bytes 221200 | tf_op jit(solution)/shard_map/reduce_scatter | solution.py:260
  (195 shorter events, 71.6 us)
Async XLA Ops:
  7.2 75.1 %copy-start = (f32[32,12]{0,1:T(8,128)S(1)}, f32[32,12]{0,1:T(8,128)}, u32[]{:S(2)}) copy-start(f32[32,12]{0,1:T(8,128)} %param.19) | copy-start | bytes 4612
  7.2 66.4 %all-gather.6.cloned.1.call-start = ((), (), s32[]{:S(2)}) async-start(), calls=%async_computation.9 | async-start | bytes 3649536 | tf_op jit(solution)/shard_map/all_gather | solution.py:92
  7.9 100.5 %all-gather.8.cloned.1.call-start = ((), (), s32[]{:S(2)}) async-start(), calls=%async_computation.10 | async-start | bytes 1966080 | tf_op jit(solution)/shard_map/all_gather | solution.py:104
  52.5 27.5 %copy-start.29 = (f32[768]{0:T(1024)}, f32[768]{0:T(1024)S(1)}, u32[]{:S(2)}) copy-start(f32[768]{0:T(1024)S(1)} %convert_element_type.196) | copy-start | bytes 9220
  53.6 26.4 %copy-start.35 = (f32[128]{0:T(128)}, f32[128]{0:T(128)S(1)}, u32[]{:S(2)}) copy-start(f32[128]{0:T(128)S(1)} %add_rsqrt_fusion.1) | copy-start | bytes 1540
  53.6 26.9 %copy-start.39 = (s32[1,128,2]{1,2,0:T(2,128)S(1)}, s32[1,128,2]{1,2,0:T(2,128)}, u32[]{:S(2)}) copy-start(s32[1,128,2]{1,2,0:T(2,128)} %param.14) | copy-start | bytes 3076
  78.7 86.6 %all-gather.10.cloned.1.call-start = ((), (), s32[]{:S(2)}) async-start(), calls=%async_computation.11 | async-start | bytes 1216512 | tf_op jit(solution)/shard_map/all_gather | solution.py:93
  79.4 143.5 %all-gather.12.cloned.1.call-start = ((), (), s32[]{:S(2)}) async-start(), calls=%async_computation.12 | async-start | bytes 5898240 | tf_op jit(solution)/shard_map/all_gather | solution.py:165
  80.0 201.5 %all-gather.14.cloned.1.call-start = ((), (), s32[]{:S(2)}) async-start(), calls=%async_computation.13 | async-start | bytes 5898240 | tf_op jit(solution)/shard_map/all_gather | solution.py:166
  95.3 20.3 %copy-start.20 = (bf16[128,768]{0,1:T(8,128)(2,1)}, bf16[128,768]{0,1:T(8,128)(2,1)S(1)}, u32[]{:S(2)}) copy-start(bf16[128,768]{0,1:T(8,128)(2,1)S(1)} %copy.48) | copy-start | bytes 589828
  95.3 20.3 %copy-start.22 = (pred[128,512]{1,0:T(8,128)(4,1)S(1)}, pred[128,512]{1,0:T(8,128)(4,1)}, u32[]{:S(2)}) copy-start(pred[128,512]{1,0:T(8,128)(4,1)} %fusion.54) | copy-start | bytes 196612
  117.7 47.6 %copy-start.7 = (f32[1,128,768]{2,1,0:T(8,128)S(1)}, f32[1,128,768]{2,1,0:T(8,128)}, u32[]{:S(2)}) copy-start(f32[1,128,768]{2,1,0:T(8,128)} %param.12) | copy-start | bytes 1179652
  119.4 47.9 %copy-start.31 = (f32[768]{0:T(1024)S(1)}, f32[768]{0:T(1024)}, u32[]{:S(2)}) copy-start(f32[768]{0:T(1024)} %convert_element_type.218) | copy-start | bytes 9220
  119.4 48.0 %copy-start.32 = (s32[1024]{0:T(1024)S(1)}, s32[1024]{0:T(1024)}, u32[]{:S(2)}) copy-start(s32[1024]{0:T(1024)} %get-tuple-element.32) | copy-start | bytes 12292
  120.2 47.1 %copy-start.24 = (bf16[12,64,128]{2,1,0:T(8,128)(2,1)}, bf16[12,64,128]{2,1,0:T(8,128)(2,1)S(1)}, u32[]{:S(2)}) copy-start(bf16[12,64,128]{2,1,0:T(8,128)(2,1)S(1)} %convolution_convert_fusion.7) | copy-start | bytes 589828
  167.2 153.2 %copy-start.10 = (f32[128,768]{1,0:T(8,128)}, f32[128,768]{1,0:T(8,128)S(1)}, u32[]{:S(2)}) copy-start(f32[128,768]{1,0:T(8,128)S(1)} %get-tuple-element.27) | copy-start | bytes 1179652
  167.3 153.2 %copy-start.37 = (f32[128]{0:T(128)}, f32[128]{0:T(128)S(1)}, u32[]{:S(2)}) copy-start(f32[128]{0:T(128)S(1)} %add_rsqrt_fusion) | copy-start | bytes 1540
  170.5 20.7 %all-to-all-start = ((bf16[8,48,768]{2,1,0:T(8,128)(2,1)}), bf16[8,48,768]{2,1,0:T(8,128)(2,1)S(1)}, u32[]{:S(2)}, u32[]{:S(2)}) async-start(bf16[8,48,768]{2,1,0:T(8,128)(2,1)} %broadcast_select_fusion), calls=%async_computation | async-start | bytes 1179648 | tf_op jit(solution)/shard_map/all_to_all | solution.py:155
  191.2 38.2 %copy-start.25 = (bf16[8,48,768]{2,1,0:T(8,128)(2,1)}, bf16[8,48,768]{2,1,0:T(8,128)(2,1)S(1)}, u32[]{:S(2)}) copy-start(bf16[8,48,768]{2,1,0:T(8,128)(2,1)S(1)} %all-to-all-done) | copy-start | bytes 1769476
  191.2 38.2 %all-to-all-start.2 = ((bf16[8,48,768]{2,1,0:T(8,128)(2,1)}), bf16[8,48,768]{2,1,0:T(8,128)(2,1)S(1)}, u32[]{:S(2)}, u32[]{:S(2)}) async-start(bf16[8,48,768]{2,1,0:T(8,128)(2,1)} %select_convert_fusion), calls=%async_computation.2 | async-start | bytes 1179648 | tf_op jit(solution)/shard_map/all_to_all | solution.py:158
  229.4 59.8 %copy-start.27 = (bf16[8,48,768]{2,1,0:T(8,128)(2,1)}, bf16[8,48,768]{2,1,0:T(8,128)(2,1)S(1)}, u32[]{:S(2)}) copy-start(bf16[8,48,768]{2,1,0:T(8,128)(2,1)S(1)} %all-to-all-done.2) | copy-start | bytes 1769476
  292.1 21.3 %all-to-all-start.3 = ((bf16[8,48,768]{2,1,0:T(8,128)(2,1)}), bf16[8,48,768]{2,1,0:T(8,128)(2,1)S(1)}, u32[]{:S(2)}, u32[]{:S(2)}) async-start(bf16[8,48,768]{2,1,0:T(8,128)(2,1)} %bitcast.25), calls=%async_computation.3 | async-start | bytes 1179648 | tf_op jit(solution)/shard_map/all_to_all | solution.py:187
  296.7 21.2 %copy-start.41 = (s32[256,1]{0,1:T(1,128)S(1)}, s32[256,1]{0,1:T(1,128)}, u32[]{:S(2)}) copy-start(s32[256,1]{0,1:T(1,128)} %copy-done.40) | copy-start | bytes 3076
  313.4 20.2 %all-to-all-start.1 = ((bf16[8,48,768]{2,1,0:T(8,128)(2,1)}), bf16[8,48,768]{2,1,0:T(8,128)(2,1)S(1)}, u32[]{:S(2)}, u32[]{:S(2)}) async-start(bf16[8,48,768]{2,1,0:T(8,128)(2,1)} %bitcast.18), calls=%async_computation.1 | async-start | bytes 1179648 | tf_op jit(solution)/shard_map/all_to_all | solution.py:180
  317.0 63.2 %reduce-scatter.16.cloned.1.call-start = ((), (), s32[]{:S(2)}) async-start(), calls=%async_computation.18 | async-start | bytes 1966080
  320.5 14.4 %copy-start.15 = (f32[128,768]{1,0:T(8,128)}, f32[128,768]{1,0:T(8,128)S(1)}, u32[]{:S(2)}) copy-start(f32[128,768]{1,0:T(8,128)S(1)} %reduce_sum.107) | copy-start | bytes 1179652
  350.9 90.6 %reduce-scatter.12.cloned.1.call-start = ((), (), s32[]{:S(2)}) async-start(), calls=%async_computation.16 | async-start | bytes 5898240 | tf_op jit(solution)/shard_map/reduce_scatter | solution.py:172
  357.0 144.5 %reduce-scatter.14.cloned.1.call-start = ((), (), s32[]{:S(2)}) async-start(), calls=%async_computation.17 | async-start | bytes 5898240 | tf_op jit(solution)/shard_map/reduce_scatter | solution.py:175
  365.6 241.4 %reduce-scatter.10.cloned.1.call-start = ((), (), s32[]{:S(2)}) async-start(), calls=%async_computation.15 | async-start | bytes 2433024 | tf_op jit(solution)/shard_map/reduce_scatter | solution.py:261
  369.6 362.1 %reduce-scatter.8.cloned.1.call-start = ((), (), s32[]{:S(2)}) async-start(), calls=%async_computation.14 | async-start | bytes 7299072 | tf_op jit(solution)/shard_map/reduce_scatter | solution.py:260
  397.1 43.0 %copy-start.13 = (f32[128,768]{1,0:T(8,128)S(1)}, f32[128,768]{1,0:T(8,128)}, u32[]{:S(2)}) copy-start(f32[128,768]{1,0:T(8,128)} %copy-done.11) | copy-start | bytes 1179652
  440.1 291.6 %copy-start.1 = (f32[32,12]{0,1:T(8,128)S(1)}, f32[32,12]{0,1:T(8,128)}, u32[]{:S(2)}) copy-start(f32[32,12]{0,1:T(8,128)} %param.19) | copy-start | bytes 4612
  (29 other events, 126.5 us)
Sparse Core Ops, SparseCore 0:
  10.9 62.6 all-gather.5
  78.8 29.6 all-gather.7
  111.3 53.9 all-gather.9
  167.0 55.8 all-gather.11
  224.5 56.9 all-gather.13
  351.0 29.0 reduce-scatter.15
  383.1 58.2 reduce-scatter.11
  444.4 56.9 reduce-scatter.13
  507.3 99.6 reduce-scatter.9
  613.1 118.4 reduce-scatter.7
where the time goes:
time: 748 us; the launch traced here: 739 us
  waiting for transfers between devices  486 us (65%)
  blocking collectives  83.8 us (11%)
  matrix products  73.1 us (10%)
  local copies, waits for them, and re-layouts  43.2 us (6%)
  other arithmetic  21.4 us (3%)
  starting transfers between devices  16.5 us (2%)
  between operations  15.1 us (2%)
    reduce_scatter x1, waiting for transfers between devices, local(): lax.psum_scatter(entry_grad, ('dp', 'seq', 'expert'), scatter_dimension=1...  125 us
    reduce_scatter x1, waiting for transfers between devices, local(): lax.psum_scatter(exit_grad, ('dp', 'seq', 'expert'), scatter_dimension=1,...  103 us
    unnamed x2, blocking collectives  83.8 us
    reduce_scatter x1, waiting for transfers between devices, local(): lax.psum_scatter(down_grad[None].astype(jnp.bfloat16), 'seq', scatter_dim...  57.2 us
    all_gather x1, waiting for transfers between devices, local(): lax.all_gather(expert_down, 'seq', axis=1, tiled=True)  52.1 us
    all_gather x1, waiting for transfers between devices, local(): lax.all_gather(exit_weight, ('dp', 'seq', 'expert'), axis=1, tiled=True)  45.1 us
    all_gather x1, waiting for transfers between devices, local(): lax.all_gather(expert_up, 'seq', axis=2, tiled=True)  28.1 us
    dot_general x4, matrix products, contract_rows(): lax.dot_general(left, right, (((0,), (0,)), ((), ())), preferred_element_...  21.7 us
  transfers between devices with their start and end apart: 14, of which 13 were waited for; matrix products, arithmetic and copies ran while one was open for 14% of the time, Pallas kernels for 0%

commit v1 on v0

--- a/solution.py
+++ b/solution.py
@@ -9,6 +9,28 @@
 LIMITS = (19, 21, 24, 27, 31, 35, 40, 46, 52, 59, 67, 77, 87, 99, 113)
 MASKED = -1e30
 HIGH = lax.Precision.HIGHEST
+
+
+def laid_out(tiles, dim):
+    tiles = jnp.moveaxis(tiles, 0, dim)
+    shape = tiles.shape
+    return tiles.reshape(*shape[:dim], shape[dim] * shape[dim + 1], *shape[dim + 2 :])
+
+
+def ring_gather(x, axis, dim):
+    count = lax.axis_size(axis)
+    pairs = [(i, (i + 1) % count) for i in range(count)]
+    back = [(b, a) for a, b in pairs]
+    lower, upper = ([], [])
+    for step in range(count - 1):
+        if step % 2 == 0:
+            lower.append(lax.ppermute(lower[-1] if lower else x, axis, pairs))
+        else:
+            upper.append(lax.ppermute(upper[-1] if upper else x, axis, back))
+    blocks = jnp.stack([*lower[::-1], x, *upper])
+    shift = lax.axis_index(axis) - len(lower)
+    blocks = blocks[(jnp.arange(count) - shift) % count]
+    return laid_out(blocks, dim)
 
 
 def gelu_value(values):
@@ -163,7 +185,7 @@
     upstream_flat = arrived_upstream.reshape(group_size * capacity, features)
     full_up, full_down = (
         lax.all_gather(expert_up, "seq", axis=2, tiled=True),
-        lax.all_gather(expert_down, "seq", axis=1, tiled=True),
+        ring_gather(expert_down, "seq", 1),
     )
     result, back_rows, up_grad, down_grad = expert_work(
         rows_flat, upstream_flat, full_up[0], full_down[0]

time: 748 us -> 723 us (0.967)
  waiting for transfers between devices: 486 us -> 427 us
  local copies, waits for them, and re-layouts: 43.2 us -> 63.8 us
  other arithmetic: 21.4 us -> 31.5 us
    reduce_scatter x1, waiting for transfers between devices: 0.44 us -> 57.2 us  [local(): lax.psum_scatter(up_grad[None].astype(jnp.bfloat16), 'seq', scatter_dimen...]
    reduce_scatter x1, waiting for transfers between devices: 57.2 us -> 0.45 us  [local(): lax.psum_scatter(down_grad[None].astype(jnp.bfloat16), 'seq', scatter_dim...]
    all_gather x1 -> x0, waiting for transfers between devices: 52.1 us -> none  [local(): lax.all_gather(expert_down, 'seq', axis=1, tiled=True)]
    ppermute x0 -> x3, waiting for transfers between devices: none -> 24.9 us  [the longest x2 24.9 us: ring_gather(): lower.append(lax.ppermute(lower[-1] if lower else x, axis, pairs))]
    all_gather x1, waiting for transfers between devices: 13.1 us -> 0.02 us  [local(): lax.all_gather(projected[:, features:], 'seq', axis=0, tiled=True)]
    all_gather x1, waiting for transfers between devices: 28.1 us -> 17 us  [local(): lax.all_gather(expert_up, 'seq', axis=2, tiled=True)]
    all_to_all x1, waiting for transfers between devices: 10.6 us -> 0.01 us  [local(): lax.all_to_all(send_rows.reshape(shaped), ('dp', 'expert'), split_axis=0,...]
    all_gather x1, waiting for transfers between devices: 45.1 us -> 55.1 us  [local(): lax.all_gather(exit_weight, ('dp', 'seq', 'expert'), axis=1, tiled=True)]
  transfers between devices with their start and end apart: 14 -> 16, of which waited for: 13 -> 11; matrix products, arithmetic and copies ran while one was open for 14% -> 18% of each run, Pallas kernels for 0% -> 0%
where the time goes in v1:
time: 723 us; the launch traced here: 713 us
  waiting for transfers between devices  427 us (59%)
  blocking collectives  83.8 us (12%)
  matrix products  69.5 us (10%)
  local copies, waits for them, and re-layouts  63.8 us (9%)
  other arithmetic  31.5 us (4%)
  starting transfers between devices  22.8 us (3%)
  between operations  14.7 us (2%)
    reduce_scatter x1, waiting for transfers between devices, local(): lax.psum_scatter(entry_grad, ('dp', 'seq', 'expert'), scatter_dimension=1...  125 us
    reduce_scatter x1, waiting for transfers between devices, local(): lax.psum_scatter(exit_grad, ('dp', 'seq', 'expert'), scatter_dimension=1,...  103 us
    unnamed x2, blocking collectives  83.8 us
    reduce_scatter x1, waiting for transfers between devices, local(): lax.psum_scatter(up_grad[None].astype(jnp.bfloat16), 'seq', scatter_dimen...  57.2 us
    all_gather x1, waiting for transfers between devices, local(): lax.all_gather(exit_weight, ('dp', 'seq', 'expert'), axis=1, tiled=True)  55.1 us
    ppermute x2, waiting for transfers between devices, ring_gather(): lower.append(lax.ppermute(lower[-1] if lower else x, axis, pairs))  24.9 us
    dot_general x4, matrix products, contract_rows(): lax.dot_general(left, right, (((0,), (0,)), ((), ())), preferred_element_...  21.4 us
    all_gather x1, waiting for transfers between devices, local(): lax.all_gather(entry_weight, ('dp', 'seq', 'expert'), axis=1, tiled=True)  20 us
  transfers between devices with their start and end apart: 16, of which 11 were waited for; matrix products, arithmetic and copies ran while one was open for 18% of the time, Pallas kernels for 0%

profile of v1, /device:TPU:0, one launch (start us, length us, event | category | flops | bytes accessed | tf_op | source)
XLA Modules:
  0.0 713.2 jit_solution(8396130288251240284)
XLA Ops:
  9.7 42.8 %all-reduce.5 = (bf16[768]{0:T(1024)(128)(2,1)S(1)}, bf16[768]{0:T(1024)(128)(2,1)S(1)}) all-reduce(bf16[768]{0:T(1024)(128)(2,1)S(1)} %dynamic-update-slice, bf16[768]{0:T(1024)(128)(2,1)S(1)} %dynamic-update-slice.1), channel_id=1, replica_groups=mesh['dp'=4,'seq'=4,'expert'=2] {'dp','seq','expert'}, use_global_device_ids=true, to_apply=%add | all-reduce | flops 1536 | bytes 6144
  53.6 20.0 %all-gather.5.cloned.1.call-done = bf16[768,2304]{0,1:T(8,128)(2,1)} async-done(((bf16[768,72]{0,1:T(8,128)(2,1)}), bf16[768,2304]{0,1:T(8,128)(2,1)}) %all-gather.5.cloned.1.call-update) | async-done | bytes 3538960 | tf_op jit(solution)/shard_map/all_gather | solution.py:114
  73.6 3.4 convolution_convert_fusion.2
  87.1 4.2 fusion.1
  91.3 5.0 copy.51
  97.0 24.9 %collective-permute-done = bf16[1,768,768]{2,1,0:T(8,128)(2,1)} collective-permute-done((bf16[1,768,768]{2,1,0:T(8,128)(2,1)}, bf16[1,768,768]{2,1,0:T(8,128)(2,1)}, u32[]{:S(2)}, u32[]{:S(2)}) %collective-permute-start) | collective-permute-done | bytes 1179680 | tf_op jit(solution)/shard_map/ppermute | solution.py:27
  132.2 55.1 %all-gather.9.cloned.1.call-done = bf16[768,768]{0,1:T(8,128)(2,1)} async-done(((bf16[768,24]{0,1:T(8,128)(2,1)}), bf16[768,768]{0,1:T(8,128)(2,1)}) %all-gather.9.cloned.1.call-update) | async-done | bytes 1179664 | tf_op jit(solution)/shard_map/all_gather | solution.py:115
  194.9 4.7 all-to-all-start
  202.0 4.1 gather_fusion.4
  212.3 4.1 maximum_bitcast_fusion
  216.4 6.3 gather_fusion.1
  222.8 5.0 all-to-all-start.2
  227.8 17.0 %all-gather.11.cloned.1.call-done = bf16[1,768,3072]{2,1,0:T(8,128)(2,1)} async-done(((bf16[1,768,768]{2,1,0:T(8,128)(2,1)}), bf16[1,768,3072]{2,1,0:T(8,128)(2,1)}) %all-gather.11.cloned.1.call-update) | async-done | bytes 4718608 | tf_op jit(solution)/shard_map/all_gather | solution.py:187
  244.9 4.7 fusion.11
  251.7 3.7 convolution_convert_fusion.5
  255.4 4.6 all-to-all-start.1
  260.0 6.6 fusion.8
  268.0 5.3 fusion.19
  273.2 3.6 all-to-all-done.1
  276.8 4.2 all-to-all-start.3
  282.6 3.3 gather_fusion.2
  285.9 11.8 %all-to-all-done.3 = bf16[8,48,768]{2,1,0:T(8,128)(2,1)} async-done(((bf16[8,48,768]{2,1,0:T(8,128)(2,1)}), bf16[8,48,768]{2,1,0:T(8,128)(2,1)}, u32[]{:S(2)}, u32[]{:S(2)}) %all-to-all-start.3) | async-done | bytes 589856 | tf_op jit(solution)/shard_map/all_to_all | solution.py:209
  325.6 7.7 %fusion.14 = bf16[1,3072,768]{2,1,0:T(8,128)(2,1)} fusion(bf16[384,768]{1,0:T(8,128)(2,1)} %bitcast.30, f32[384,3072]{1,0:T(8,128)} %copy-done.37), kind=kOutput, calls=%fused_computation.28 | convolution fusion | flops 1824915456 | bytes 10027008 | tf_op jit(solution)/shard_map/dot_general | solution.py:59
  335.0 5.6 fusion.13
  347.2 7.6 %reduce-scatter.16.cloned.1.call-done = bf16[128,1536]{1,0:T(8,128)(2,1)} async-done(((bf16[512,1536]{1,0:T(8,128)(2,1)}), bf16[128,1536]{1,0:T(8,128)(2,1)}) %reduce-scatter.16.cloned.1.call-update) | async-done | bytes 393232
  356.7 5.0 fusion.27
  361.8 3.5 copy.58
  365.3 6.3 fusion.22
  372.5 41.0 %all-reduce.4 = (f32[768]{0:T(1024)S(1)}, f32[32,12]{0,1:T(8,128)}, f32[768]{0:T(1024)S(1)}) all-reduce(f32[768]{0:T(1024)S(1)} %get-tuple-element.11, f32[32,12]{0,1:T(8,128)S(1)} %fusion.22, f32[768]{0:T(1024)S(1)} %copy-done.28), channel_id=3, replica_groups=mesh['dp'=4,'seq'=4,'expert'=2] {'dp','seq','expert'}, use_global_device_ids=true, to_apply=%region_15.16.clone | all-reduce | flops 1920 | bytes 15360
  418.9 57.2 %reduce-scatter.12.cloned.1.call-done = bf16[1,768,768]{2,1,0:T(8,128)(2,1)} async-done(((bf16[1,768,3072]{2,1,0:T(8,128)(2,1)}), bf16[1,768,768]{2,1,0:T(8,128)(2,1)}) %reduce-scatter.12.cloned.1.call-update) | async-done | bytes 1179664 | tf_op jit(solution)/shard_map/reduce_scatter | solution.py:194
  478.9 102.6 %reduce-scatter.10.cloned.1.call-done = f32[768,24]{0,1:T(8,128)} async-done(((f32[768,768]{0,1:T(8,128)}), f32[768,24]{0,1:T(8,128)}) %reduce-scatter.10.cloned.1.call-update) | async-done | bytes 73744 | tf_op jit(solution)/shard_map/reduce_scatter | solution.py:283
  581.5 124.9 %reduce-scatter.8.cloned.1.call-done = f32[768,72]{0,1:T(8,128)} async-done(((f32[768,2304]{0,1:T(8,128)}), f32[768,72]{0,1:T(8,128)}) %reduce-scatter.8.cloned.1.call-update) | async-done | bytes 221200 | tf_op jit(solution)/shard_map/reduce_scatter | solution.py:282
  (189 shorter events, 92.8 us)
Async XLA Ops:
  7.2 79.9 %copy-start = (f32[32,12]{0,1:T(8,128)S(1)}, f32[32,12]{0,1:T(8,128)}, u32[]{:S(2)}) copy-start(f32[32,12]{0,1:T(8,128)} %param.19) | copy-start | bytes 4612
  7.2 66.4 %all-gather.5.cloned.1.call-start = ((), (), s32[]{:S(2)}) async-start(), calls=%async_computation.9 | async-start | bytes 3649536 | tf_op jit(solution)/shard_map/all_gather | solution.py:114
  7.9 114.7 %all-gather.7.cloned.1.call-start = ((), (), s32[]{:S(2)}) async-start(), calls=%async_computation.10 | async-start | bytes 1966080 | tf_op jit(solution)/shard_map/all_gather | solution.py:126
  52.5 26.7 %copy-start.24 = (f32[768]{0:T(1024)}, f32[768]{0:T(1024)S(1)}, u32[]{:S(2)}) copy-start(f32[768]{0:T(1024)S(1)} %convert_element_type.196) | copy-start | bytes 9220
  53.6 25.5 %copy-start.29 = (f32[128]{0:T(128)}, f32[128]{0:T(128)S(1)}, u32[]{:S(2)}) copy-start(f32[128]{0:T(128)S(1)} %add_rsqrt_fusion.1) | copy-start | bytes 1540
  53.6 28.5 %copy-start.34 = (s32[1,128,2]{1,2,0:T(2,128)S(1)}, s32[1,128,2]{1,2,0:T(2,128)}, u32[]{:S(2)}) copy-start(s32[1,128,2]{1,2,0:T(2,128)} %param.14) | copy-start | bytes 3076
  77.8 109.5 %all-gather.9.cloned.1.call-start = ((), (), s32[]{:S(2)}) async-start(), calls=%async_computation.11 | async-start | bytes 1216512 | tf_op jit(solution)/shard_map/all_gather | solution.py:115
  78.6 166.3 %all-gather.11.cloned.1.call-start = ((), (), s32[]{:S(2)}) async-start(), calls=%async_computation.12 | async-start | bytes 5898240 | tf_op jit(solution)/shard_map/all_gather | solution.py:187
  79.2 42.7 %collective-permute-start = (bf16[1,768,768]{2,1,0:T(8,128)(2,1)}, bf16[1,768,768]{2,1,0:T(8,128)(2,1)}, u32[]{:S(2)}, u32[]{:S(2)}) collective-permute-start(bf16[1,768,768]{2,1,0:T(8,128)(2,1)} %param.22), channel_id=1, source_target_pairs={{0,2},{2,4},{4,6},{6,0},{1,3},{3,5},{5,7},{7,1},{8,10},{10,12},{12... | collective-permute-start | bytes 3538952 | tf_op jit(solution)/shard_map/ppermute | solution.py:27
  80.6 131.7 %collective-permute-start.2 = (bf16[1,768,768]{2,1,0:T(8,128)(2,1)}, bf16[1,768,768]{2,1,0:T(8,128)(2,1)}, u32[]{:S(2)}, u32[]{:S(2)}) collective-permute-start(bf16[1,768,768]{2,1,0:T(8,128)(2,1)} %param.22), channel_id=1, source_target_pairs={{2,0},{4,2},{6,4},{0,6},{3,1},{5,3},{7,5},{1,7},{10,8},{12,10},{14... | collective-permute-start | bytes 3538952 | tf_op jit(solution)/shard_map/ppermute | solution.py:29
  97.0 29.5 %copy-start.21 = (pred[128,512]{1,0:T(8,128)(4,1)}, pred[128,512]{1,0:T(8,128)(4,1)S(1)}, u32[]{:S(2)}) copy-start(pred[128,512]{1,0:T(8,128)(4,1)S(1)} %fusion.45) | copy-start | bytes 196612
  121.9 90.4 %collective-permute-start.1 = (bf16[1,768,768]{2,1,0:T(8,128)(2,1)}, bf16[1,768,768]{2,1,0:T(8,128)(2,1)}, u32[]{:S(2)}, u32[]{:S(2)}) collective-permute-start(bf16[1,768,768]{2,1,0:T(8,128)(2,1)} %collective-permute-done), channel_id=1, source_target_pairs={{0,2},{2,4},{4,6},{6,0},{1,3},{3,5},{5,7},{7,1},{8,10},{10,12},{12... | collective-permute-start | bytes 3538952 | tf_op jit(solution)/shard_map/ppermute | solution.py:27
  129.5 57.8 %copy-start.5 = (f32[1,128,768]{2,1,0:T(8,128)S(1)}, f32[1,128,768]{2,1,0:T(8,128)}, u32[]{:S(2)}) copy-start(f32[1,128,768]{2,1,0:T(8,128)} %param.12) | copy-start | bytes 1179652
  130.7 59.4 %copy-start.26 = (f32[768]{0:T(1024)S(1)}, f32[768]{0:T(1024)}, u32[]{:S(2)}) copy-start(f32[768]{0:T(1024)} %convert_element_type.218) | copy-start | bytes 9220
  130.7 59.5 %copy-start.27 = (s32[1024]{0:T(1024)S(1)}, s32[1024]{0:T(1024)}, u32[]{:S(2)}) copy-start(s32[1024]{0:T(1024)} %get-tuple-element.32) | copy-start | bytes 12292
  192.8 14.0 %copy-start.2 = (f32[1,128,768]{2,1,0:T(8,128)S(1)}, f32[1,128,768]{2,1,0:T(8,128)}, u32[]{:S(2)}) copy-start(f32[1,128,768]{2,1,0:T(8,128)} %param.23) | copy-start | bytes 1179652
  194.9 27.8 %all-to-all-start = ((bf16[8,48,768]{2,1,0:T(8,128)(2,1)}), bf16[8,48,768]{2,1,0:T(8,128)(2,1)}, u32[]{:S(2)}, u32[]{:S(2)}) async-start(bf16[8,48,768]{2,1,0:T(8,128)(2,1)} %broadcast_select_fusion), calls=%async_computation | async-start | bytes 1179648 | tf_op jit(solution)/shard_map/all_to_all | solution.py:177
  222.8 32.6 %all-to-all-start.2 = ((bf16[8,48,768]{2,1,0:T(8,128)(2,1)}), bf16[8,48,768]{2,1,0:T(8,128)(2,1)}, u32[]{:S(2)}, u32[]{:S(2)}) async-start(bf16[8,48,768]{2,1,0:T(8,128)(2,1)} %select_convert_fusion), calls=%async_computation.2 | async-start | bytes 1179648 | tf_op jit(solution)/shard_map/all_to_all | solution.py:180
  255.4 21.4 %all-to-all-start.1 = ((bf16[8,48,768]{2,1,0:T(8,128)(2,1)}), bf16[8,48,768]{2,1,0:T(8,128)(2,1)}, u32[]{:S(2)}, u32[]{:S(2)}) async-start(bf16[8,48,768]{2,1,0:T(8,128)(2,1)} %bitcast.136), calls=%async_computation.1 | async-start | bytes 1179648 | tf_op jit(solution)/shard_map/all_to_all | solution.py:202
  268.0 13.3 %copy-start.33 = (f32[1,128,2]{1,2,0:T(2,128)S(1)}, f32[1,128,2]{1,2,0:T(2,128)}, u32[]{:S(2)}) copy-start(f32[1,128,2]{1,2,0:T(2,128)} %param.15) | copy-start | bytes 3076
  276.8 20.9 %all-to-all-start.3 = ((bf16[8,48,768]{2,1,0:T(8,128)(2,1)}), bf16[8,48,768]{2,1,0:T(8,128)(2,1)}, u32[]{:S(2)}, u32[]{:S(2)}) async-start(bf16[8,48,768]{2,1,0:T(8,128)(2,1)} %bitcast.135), calls=%async_computation.3 | async-start | bytes 1179648 | tf_op jit(solution)/shard_map/all_to_all | solution.py:209
  281.0 73.8 %reduce-scatter.16.cloned.1.call-start = ((), (), s32[]{:S(2)}) async-start(), calls=%async_computation.17 | async-start | bytes 1966080
  301.1 11.9 %copy-start.32 = (f32[128]{0:T(128)S(1)}, f32[128]{0:T(128)}, u32[]{:S(2)}) copy-start(f32[128]{0:T(128)} %copy-done.31) | copy-start | bytes 1540
  325.6 90.4 %reduce-scatter.14.cloned.1.call-start = ((), (), s32[]{:S(2)}) async-start(), calls=%async_computation.16 | async-start | bytes 5898240 | tf_op jit(solution)/shard_map/reduce_scatter | solution.py:197
  333.4 142.7 %reduce-scatter.12.cloned.1.call-start = ((), (), s32[]{:S(2)}) async-start(), calls=%async_computation.15 | async-start | bytes 5898240 | tf_op jit(solution)/shard_map/reduce_scatter | solution.py:194
  340.6 240.9 %reduce-scatter.10.cloned.1.call-start = ((), (), s32[]{:S(2)}) async-start(), calls=%async_computation.14 | async-start | bytes 2433024 | tf_op jit(solution)/shard_map/reduce_scatter | solution.py:283
  344.6 12.1 %copy-start.6 = (f32[1,128,768]{2,1,0:T(8,128)S(1)}, f32[1,128,768]{2,1,0:T(8,128)}, u32[]{:S(2)}) copy-start(f32[1,128,768]{2,1,0:T(8,128)} %param.12) | copy-start | bytes 1179652
  344.6 12.1 %copy-start.25 = (f32[768]{0:T(1024)S(1)}, f32[768]{0:T(1024)}, u32[]{:S(2)}) copy-start(f32[768]{0:T(1024)} %copy-done.24) | copy-start | bytes 9220
  344.6 12.1 %copy-start.30 = (f32[128]{0:T(128)S(1)}, f32[128]{0:T(128)}, u32[]{:S(2)}) copy-start(f32[128]{0:T(128)} %copy-done.29) | copy-start | bytes 1540
  344.7 361.7 %reduce-scatter.8.cloned.1.call-start = ((), (), s32[]{:S(2)}) async-start(), calls=%async_computation.13 | async-start | bytes 7299072 | tf_op jit(solution)/shard_map/reduce_scatter | solution.py:282
  371.7 43.0 %copy-start.11 = (f32[128,768]{1,0:T(8,128)S(1)}, f32[128,768]{1,0:T(8,128)}, u32[]{:S(2)}) copy-start(f32[128,768]{1,0:T(8,128)} %copy-done.9) | copy-start | bytes 1179652
  414.7 291.7 %copy-start.1 = (f32[32,12]{0,1:T(8,128)S(1)}, f32[32,12]{0,1:T(8,128)}, u32[]{:S(2)}) copy-start(f32[32,12]{0,1:T(8,128)} %param.19) | copy-start | bytes 4612
  (24 other events, 76.7 us)
Sparse Core Ops, SparseCore 0:
  10.9 62.6 all-gather.4
  78.0 42.8 all-gather.6
  123.7 63.5 all-gather.8
  189.0 55.8 all-gather.10
  325.7 29.0 reduce-scatter.15
  357.7 58.3 reduce-scatter.13
  419.0 56.9 reduce-scatter.11
  481.9 99.5 reduce-scatter.9
  587.8 118.5 reduce-scatter.7
